TPU v7x, 256 devices: a whole 4x4x8 slice. The times are simulated.
256 devices in a mesh: row: 32 (over z_lo, x, core), col: 8 (over z_hi, y).
Axes of the slice: x: 4, y: 4, z: 8 (z_hi: 2, z_lo: 4; z = z_hi * 4 + z_lo), core: 2. Of those that a mesh axis runs over, the one named last changes fastest.
Arguments:
- pair: bfloat16 [512, 512, 128], P('row', 'col'), may hold values from -6 to 6
- cotangent: bfloat16 [64, 512, 512], P(None, 'row', 'col'), may hold values from -0.59765625 to 0.59765625
- w_left: bfloat16 [128, 64], replicated, may hold values from -0.5 to 0.5
- w_left_gate: bfloat16 [128, 64], replicated, may hold values from -0.5 to 0.5
- w_right: bfloat16 [128, 64], replicated, may hold values from -0.5 to 0.5
- w_right_gate: bfloat16 [128, 64], replicated, may hold values from -0.5 to 0.5
Outputs:
- pair_gradient: bfloat16 [512, 512, 128], P('row', 'col')
- grad_left: float32 [128, 64], replicated
- grad_left_gate: float32 [128, 64], replicated
- grad_right: float32 [128, 64], replicated
- grad_right_gate: float32 [128, 64], replicated
All inputs are finite; a program needn't handle non-finite values.
Results may differ from a plain program's by a relative error of at most 0.0082.
Values may be sent and summed in bfloat16 or wider, within the bound.
A program may use at most 64 MiB of HBM per device.

v0:
```python
import jax
import jax.numpy as jnp
from jax import lax
from jax.sharding import PartitionSpec as P


def shards(pair, cotangent, w_left, w_left_gate, w_right, w_right_gate):
    pair_f = pair.astype(jnp.float32)
    average = jnp.mean(pair_f, axis=-1, keepdims=True)
    centered_input = pair_f - average
    variance = jnp.mean(centered_input * centered_input, axis=-1, keepdims=True)
    inverse_scale = 1.0 / jnp.sqrt(variance + 1e-05)
    standardized_input = centered_input * inverse_scale
    normalized_input = standardized_input.astype(jnp.bfloat16)
    stacked = jnp.concatenate([w_left, w_left_gate, w_right, w_right_gate], axis=1)
    projected = jnp.einsum(
        "rcd,dh->hrc", normalized_input, stacked, preferred_element_type=jnp.float32
    )
    q_left, p_left, q_right, p_right = jnp.split(projected, 4, axis=0)
    s_left = jax.nn.sigmoid(p_left)
    s_right = jax.nn.sigmoid(p_right)
    left = (s_left * q_left).astype(jnp.bfloat16)
    right = (s_right * q_right).astype(jnp.bfloat16)
    g_chan, left_chan, right_chan = (
        lax.all_to_all(cotangent, "col", split_axis=0, concat_axis=2, tiled=True),
        lax.all_to_all(left, "col", split_axis=0, concat_axis=2, tiled=True),
        lax.all_to_all(right, "col", split_axis=0, concat_axis=2, tiled=True),
    )
    residues = g_chan.shape[2]
    col_block = g_chan
    d_left = jnp.einsum(
        "hij,hjk->hik",
        col_block,
        lax.all_gather(right_chan, "row", axis=1, tiled=True),
        preferred_element_type=jnp.float32,
    )
    col_block = g_chan
    summed = lax.psum_scatter(
        jnp.einsum("hij,hik->jhk", col_block, left_chan, preferred_element_type=jnp.float32),
        "row",
        scatter_dimension=0,
        tiled=True,
    )
    d_right = jnp.transpose(summed, (1, 0, 2))
    d_left_tile, d_right_tile = (
        lax.all_to_all(d_left.astype(jnp.bfloat16), "col", split_axis=2, concat_axis=0, tiled=True),
        lax.all_to_all(
            d_right.astype(jnp.bfloat16), "col", split_axis=2, concat_axis=0, tiled=True
        ),
    )
    grad_l = d_left_tile.astype(jnp.float32)
    grad_r = d_right_tile.astype(jnp.float32)
    e_left = grad_l * s_left
    f_left = grad_l * q_left * s_left * (1.0 - s_left)
    e_right = grad_r * s_right
    f_right = grad_r * q_right * s_right * (1.0 - s_right)
    grads = jnp.concatenate([e_left, f_left, e_right, f_right], axis=0).astype(jnp.bfloat16)
    local_weights = jnp.einsum(
        "rcd,hrc->dh", normalized_input, grads, preferred_element_type=jnp.float32
    )
    total_weights = lax.psum(local_weights, ("row", "col")) / residues
    normalized_gradient = jnp.einsum(
        "hrc,dh->rcd", grads, stacked, preferred_element_type=jnp.float32
    )
    gradient_mean = jnp.mean(normalized_gradient, axis=-1, keepdims=True)
    gradient_input_mean = jnp.mean(normalized_gradient * standardized_input, axis=-1, keepdims=True)
    pair_gradient = (
        (normalized_gradient - gradient_mean - standardized_input * gradient_input_mean)
        * inverse_scale
    ).astype(jnp.bfloat16)
    pieces_w = jnp.split(total_weights, 4, axis=1)
    return (pair_gradient, pieces_w[0], pieces_w[1], pieces_w[2], pieces_w[3])


def solution(mesh):
    in_specs = (P("row", "col", None), P(None, "row", "col"), P(), P(), P(), P())
    out_specs = (P("row", "col", None), P(), P(), P(), P())
    return jax.shard_map(shards, mesh=mesh, in_specs=in_specs, out_specs=out_specs, check_vma=False)
```

profile of v0, /device:TPU:2, one launch (start us, length us, event | category | flops | bytes accessed | tf_op | source)
XLA Modules:
  0.0 579.7 jit_solution(9537658770375944991)
XLA Ops:
  7.2 1.2 convert_reduce_fusion
  8.4 1.3 fusion.10
  9.8 0.8 copy.87
  10.6 0.8 copy.88
  11.4 0.8 copy.89
  12.3 0.8 copy.90
  13.1 1.4 fusion.18
  15.3 21.4 %all_to_all.72 = bf16[8,2,4096]{2,1,0:T(2,128)(2,1)S(1)} all-to-all(bf16[8,2,4096]{2,1,0:T(2,128)(2,1)S(1)} %reshape.47), channel_id=1, replica_groups=mesh['row'=32,'col'=8] {'col'}, dimensions={0} | all-to-all | bytes 262144 | tf_op jit(solution)/shard_map/all_to_all | solution.py:27
  37.1 0.9 all_to_all.56
  38.3 13.0 %all_to_all.73 = bf16[8,2,4096]{2,1,0:T(2,128)(2,1)S(1)} all-to-all(bf16[8,2,4096]{2,1,0:T(2,128)(2,1)S(1)} %reshape.45), channel_id=1, replica_groups=mesh['row'=32,'col'=8] {'col'}, dimensions={0} | all-to-all | bytes 262144 | tf_op jit(solution)/shard_map/all_to_all | solution.py:25
  51.9 43.9 %all-gather.2.cloned.1.call-done = bf16[8,512,512]{2,1,0:T(8,128)(2,1)} async-done(((bf16[8,16,512]{2,1,0:T(8,128)(2,1)}), bf16[8,512,512]{2,1,0:T(8,128)(2,1)}) %all-gather.2.cloned.1.call-update) | async-done | bytes 4194320 | tf_op jit(solution)/shard_map/all_gather | solution.py:34
  95.9 2.8 fusion
  98.7 0.8 copy.94
  99.5 1.1 reshape.49
  100.5 18.0 %all_to_all.74 = bf16[8,2,4096]{2,1,0:T(2,128)(2,1)S(1)} all-to-all(bf16[8,2,4096]{2,1,0:T(2,128)(2,1)S(1)} %reshape.49), channel_id=1, replica_groups=mesh['row'=32,'col'=8] {'col'}, dimensions={0} | all-to-all | bytes 262144 | tf_op jit(solution)/shard_map/all_to_all | solution.py:46
  118.6 0.7 reshape.50
  119.3 0.7 copy.95
  121.4 13.0 %all_to_all.75 = bf16[8,2,4096]{2,1,0:T(2,128)(2,1)S(1)} all-to-all(bf16[8,2,4096]{2,1,0:T(2,128)(2,1)S(1)} %reshape.51), channel_id=1, replica_groups=mesh['row'=32,'col'=8] {'col'}, dimensions={0} | all-to-all | bytes 262144 | tf_op jit(solution)/shard_map/all_to_all | solution.py:26
  135.1 4.5 convolution_bitcast_fusion
  139.6 10.4 %copy.101 = f32[512,8,512]{2,1,0:T(8,128)} copy(f32[512,8,512]{0,2,1:T(8,128)} %convolution_bitcast_fusion) | data formatting | bytes 16777216 | tf_op jit(solution)/shard_map/hij,hik->jhk/transpose | solution.py:39
  150.1 150.5 %reduce-scatter.2.cloned.1.call-done = f32[16,8,512]{2,1,0:T(8,128)} async-done(((f32[512,8,512]{2,1,0:T(8,128)}), f32[16,8,512]{2,1,0:T(8,128)}) %reduce-scatter.2.cloned.1.call-update) | async-done | bytes 262160 | tf_op jit(solution)/shard_map/reduce_scatter | solution.py:38
  300.5 1.0 convert_bitcast_fusion
  301.5 0.8 copy.102
  302.3 1.1 reshape.53
  303.4 16.3 %all_to_all.76 = bf16[8,2,4096]{2,1,0:T(2,128)(2,1)S(1)} all-to-all(bf16[8,2,4096]{2,1,0:T(2,128)(2,1)S(1)} %reshape.53), channel_id=1, replica_groups=mesh['row'=32,'col'=8] {'col'}, dimensions={0} | all-to-all | bytes 262144 | tf_op jit(solution)/shard_map/all_to_all | solution.py:47
  320.4 0.7 copy.103
  322.0 1.5 convolution_bitcast_fusion.1
  323.5 1.0 fusion.21
  324.5 1.3 fusion.9
  325.9 243.5 %all-reduce.2.cloned.1.call-done = f32[128,256]{1,0:T(8,128)} async-done(((f32[128,256]{1,0:T(8,128)}), f32[128,256]{1,0:T(8,128)}) %all-reduce.2.cloned.1.call-update) | async-done | bytes 131088 | tf_op jit(solution)/shard_map/psum | solution.py:61
  569.4 0.9 broadcast_multiply_fusion
  570.4 0.7 copy.110
  (40 shorter events, 7.8 us)
Async XLA Ops:
  7.2 30.9 %copy-start.1 = (bf16[64,16,64]{2,1,0:T(8,128)(2,1)S(1)}, bf16[64,16,64]{2,1,0:T(8,128)(2,1)}, u32[]{:S(2)}) copy-start(bf16[64,16,64]{2,1,0:T(8,128)(2,1)} %param.7) | copy-start | bytes 393220
  7.2 88.7 %all-gather.2.cloned.1.call-start = ((), (), s32[]{:S(2)}) async-start(), calls=%async_computation.6 | async-start | bytes 4325376 | tf_op jit(solution)/shard_map/all_gather | solution.py:34
  38.0 262.5 %reduce-scatter.2.cloned.1.call-start = ((), (), s32[]{:S(2)}) async-start(), calls=%async_computation.7 | async-start | bytes 8650752 | tf_op jit(solution)/shard_map/reduce_scatter | solution.py:38
  150.0 419.4 %all-reduce.2.cloned.1.call-start = ((), (), s32[]{:S(2)}) async-start(), calls=%async_computation.8 | async-start | bytes 262144 | tf_op jit(solution)/shard_map/psum | solution.py:61
  302.3 19.7 %copy-start = (bf16[16,64,128]{2,1,0:T(8,128)(2,1)S(1)}, bf16[16,64,128]{2,1,0:T(8,128)(2,1)}, u32[]{:S(2)}) copy-start(bf16[16,64,128]{2,1,0:T(8,128)(2,1)} %param.6) | copy-start | bytes 786436
Sparse Core Ops, SparseCore 0:
  38.1 57.7 all-gather.1
  150.1 150.3 reduce-scatter.1
  324.7 244.7 all-reduce.1
where the time goes:
time: 581 us; the launch traced here: 580 us
  waiting for transfers between devices  438 us (75%)
  blocking collectives  81.8 us (14%)
  local copies, waits for them, and re-layouts  27.9 us (5%)
  between operations  14 us (2%)
  matrix products  11.3 us (2%)
  other arithmetic  6.66 us (1%)
    psum x1, waiting for transfers between devices, shards(): total_weights = lax.psum(local_weights, ('row', 'col')) / residues  244 us
    reduce_scatter x1, waiting for transfers between devices, shards(): lax.psum_scatter(jnp.einsum('hij,hik->jhk', col_block, left_chan, preferr...  150 us
    all_gather x1, waiting for transfers between devices, shards(): lax.all_gather(right_chan, 'row', axis=1, tiled=True)  43.9 us
    all_to_all x1, blocking collectives, shards(): lax.all_to_all(right, 'col', split_axis=0, concat_axis=2, tiled=True)  21.4 us
    all_to_all x1, blocking collectives, shards(): lax.all_to_all(d_left.astype(jnp.bfloat16), 'col', split_axis=2, concat_a...  18 us
    all_to_all x1, blocking collectives, shards(): lax.all_to_all(d_right.astype(jnp.bfloat16), 'col', split_axis=2, concat_...  16.3 us
    all_to_all x1, blocking collectives, shards(): lax.all_to_all(left, 'col', split_axis=0, concat_axis=2, tiled=True)  13 us
    all_to_all x1, blocking collectives, shards(): lax.all_to_all(cotangent, 'col', split_axis=0, concat_axis=2, tiled=True)  13 us
  transfers between devices with their start and end apart: 3, of which 3 were waited for; matrix products, arithmetic and copies ran while one was open for 0% of the time, Pallas kernels for 0%

commit v1 on v0

--- a/solution.py
+++ b/solution.py
@@ -58,7 +58,7 @@
     local_weights = jnp.einsum(
         "rcd,hrc->dh", normalized_input, grads, preferred_element_type=jnp.float32
     )
-    total_weights = lax.psum(local_weights, ("row", "col")) / residues
+    total_weights = lax.psum(lax.psum(local_weights, "col"), "row") / residues
     normalized_gradient = jnp.einsum(
         "hrc,dh->rcd", grads, stacked, preferred_element_type=jnp.float32
     )

time: 581 us -> 696 us (1.20)
  waiting for transfers between devices: 438 us -> 549 us
    psum x1 -> x2, waiting for transfers between devices: 244 us -> 355 us  [shards(): total_weights = lax.psum(lax.psum(local_weights, 'col'), 'row') / residues]
  transfers between devices with their start and end apart: 3 -> 4, of which waited for: 3 -> 4; matrix products, arithmetic and copies ran while one was open for 0% -> 0% of each run, Pallas kernels for 0% -> 0%
where the time goes in v1:
time: 696 us; the launch traced here: 691 us
  waiting for transfers between devices  549 us (79%)
  blocking collectives  81.8 us (12%)
  local copies, waits for them, and re-layouts  27.9 us (4%)
  between operations  14 us (2%)
  matrix products  11.3 us (2%)
    psum x2, waiting for transfers between devices, shards(): total_weights = lax.psum(lax.psum(local_weights, 'col'), 'row') / residues  355 us
    reduce_scatter x1, waiting for transfers between devices, shards(): lax.psum_scatter(jnp.einsum('hij,hik->jhk', col_block, left_chan, preferr...  150 us
    all_gather x1, waiting for transfers between devices, shards(): lax.all_gather(right_chan, 'row', axis=1, tiled=True)  43.9 us
    all_to_all x1, blocking collectives, shards(): lax.all_to_all(right, 'col', split_axis=0, concat_axis=2, tiled=True)  21.4 us
    all_to_all x1, blocking collectives, shards(): lax.all_to_all(d_left.astype(jnp.bfloat16), 'col', split_axis=2, concat_a...  18 us
    all_to_all x1, blocking collectives, shards(): lax.all_to_all(d_right.astype(jnp.bfloat16), 'col', split_axis=2, concat_...  16.3 us
  transfers between devices with their start and end apart: 4, of which 4 were waited for; matrix products, arithmetic and copies ran while one was open for 0% of the time, Pallas kernels for 0%

profile of v1, /device:TPU:2, one launch (start us, length us, event | category | flops | bytes accessed | tf_op | source)
XLA Modules:
  0.0 691.2 jit_solution(825061688065287500)
XLA Ops:
  7.2 1.2 convert_reduce_fusion
  8.4 1.3 fusion.10
  9.8 0.8 copy.87
  10.6 0.8 copy.88
  11.4 0.8 copy.89
  12.3 0.8 copy.90
  13.1 1.4 fusion.18
  15.3 21.4 %all_to_all.72 = bf16[8,2,4096]{2,1,0:T(2,128)(2,1)S(1)} all-to-all(bf16[8,2,4096]{2,1,0:T(2,128)(2,1)S(1)} %reshape.47), channel_id=1, replica_groups=mesh['row'=32,'col'=8] {'col'}, dimensions={0} | all-to-all | bytes 262144 | tf_op jit(solution)/shard_map/all_to_all | solution.py:27
  37.1 0.9 all_to_all.56
  38.3 13.0 %all_to_all.73 = bf16[8,2,4096]{2,1,0:T(2,128)(2,1)S(1)} all-to-all(bf16[8,2,4096]{2,1,0:T(2,128)(2,1)S(1)} %reshape.45), channel_id=1, replica_groups=mesh['row'=32,'col'=8] {'col'}, dimensions={0} | all-to-all | bytes 262144 | tf_op jit(solution)/shard_map/all_to_all | solution.py:25
  51.9 43.9 %all-gather.2.cloned.1.call-done = bf16[8,512,512]{2,1,0:T(8,128)(2,1)} async-done(((bf16[8,16,512]{2,1,0:T(8,128)(2,1)}), bf16[8,512,512]{2,1,0:T(8,128)(2,1)}) %all-gather.2.cloned.1.call-update) | async-done | bytes 4194320 | tf_op jit(solution)/shard_map/all_gather | solution.py:34
  95.9 2.8 fusion
  98.7 0.8 copy.94
  99.5 1.1 reshape.49
  100.5 18.0 %all_to_all.74 = bf16[8,2,4096]{2,1,0:T(2,128)(2,1)S(1)} all-to-all(bf16[8,2,4096]{2,1,0:T(2,128)(2,1)S(1)} %reshape.49), channel_id=1, replica_groups=mesh['row'=32,'col'=8] {'col'}, dimensions={0} | all-to-all | bytes 262144 | tf_op jit(solution)/shard_map/all_to_all | solution.py:46
  119.3 0.7 copy.95
  121.4 13.0 %all_to_all.75 = bf16[8,2,4096]{2,1,0:T(2,128)(2,1)S(1)} all-to-all(bf16[8,2,4096]{2,1,0:T(2,128)(2,1)S(1)} %reshape.51), channel_id=1, replica_groups=mesh['row'=32,'col'=8] {'col'}, dimensions={0} | all-to-all | bytes 262144 | tf_op jit(solution)/shard_map/all_to_all | solution.py:26
  135.1 4.5 convolution_bitcast_fusion
  139.6 10.4 %copy.101 = f32[512,8,512]{2,1,0:T(8,128)} copy(f32[512,8,512]{0,2,1:T(8,128)} %convolution_bitcast_fusion) | data formatting | bytes 16777216 | tf_op jit(solution)/shard_map/hij,hik->jhk/transpose | solution.py:39
  150.1 150.5 %reduce-scatter.2.cloned.1.call-done = f32[16,8,512]{2,1,0:T(8,128)} async-done(((f32[512,8,512]{2,1,0:T(8,128)}), f32[16,8,512]{2,1,0:T(8,128)}) %reduce-scatter.2.cloned.1.call-update) | async-done | bytes 262160 | tf_op jit(solution)/shard_map/reduce_scatter | solution.py:38
  300.5 1.0 convert_bitcast_fusion
  301.5 0.8 copy.102
  302.3 1.1 reshape.53
  303.4 16.3 %all_to_all.76 = bf16[8,2,4096]{2,1,0:T(2,128)(2,1)S(1)} all-to-all(bf16[8,2,4096]{2,1,0:T(2,128)(2,1)S(1)} %reshape.53), channel_id=1, replica_groups=mesh['row'=32,'col'=8] {'col'}, dimensions={0} | all-to-all | bytes 262144 | tf_op jit(solution)/shard_map/all_to_all | solution.py:47
  320.4 0.7 copy.103
  322.0 1.5 convolution_bitcast_fusion.1
  323.5 1.0 fusion.21
  324.6 105.9 %all-reduce.3.cloned.1.call-done = f32[128,256]{1,0:T(8,128)} async-done(((f32[128,256]{1,0:T(8,128)}), f32[128,256]{1,0:T(8,128)}) %all-reduce.3.cloned.1.call-update) | async-done | bytes 131088 | tf_op jit(solution)/shard_map/psum | solution.py:61
  430.5 1.3 fusion.9
  431.8 249.1 %all-reduce.5.cloned.1.call-done = f32[128,256]{1,0:T(8,128)} async-done(((f32[128,256]{1,0:T(8,128)}), f32[128,256]{1,0:T(8,128)}) %all-reduce.5.cloned.1.call-update) | async-done | bytes 131088 | tf_op jit(solution)/shard_map/psum | solution.py:61
  680.9 0.9 broadcast_multiply_fusion
  681.9 0.7 copy.110
  (43 shorter events, 8.6 us)
Async XLA Ops:
  7.2 30.9 %copy-start.1 = (bf16[64,16,64]{2,1,0:T(8,128)(2,1)S(1)}, bf16[64,16,64]{2,1,0:T(8,128)(2,1)}, u32[]{:S(2)}) copy-start(bf16[64,16,64]{2,1,0:T(8,128)(2,1)} %param.7) | copy-start | bytes 393220
  7.2 88.7 %all-gather.2.cloned.1.call-start = ((), (), s32[]{:S(2)}) async-start(), calls=%async_computation.6 | async-start | bytes 4325376 | tf_op jit(solution)/shard_map/all_gather | solution.py:34
  38.0 262.5 %reduce-scatter.2.cloned.1.call-start = ((), (), s32[]{:S(2)}) async-start(), calls=%async_computation.7 | async-start | bytes 8650752 | tf_op jit(solution)/shard_map/reduce_scatter | solution.py:38
  150.0 280.5 %all-reduce.3.cloned.1.call-start = ((), (), s32[]{:S(2)}) async-start(), calls=%async_computation.8 | async-start | bytes 262144 | tf_op jit(solution)/shard_map/psum | solution.py:61
  302.3 19.7 %copy-start = (bf16[16,64,128]{2,1,0:T(8,128)(2,1)S(1)}, bf16[16,64,128]{2,1,0:T(8,128)(2,1)}, u32[]{:S(2)}) copy-start(bf16[16,64,128]{2,1,0:T(8,128)(2,1)} %param.6) | copy-start | bytes 786436
  324.5 356.4 %all-reduce.5.cloned.1.call-start = ((), (), s32[]{:S(2)}) async-start(), calls=%async_computation.9 | async-start | bytes 262144 | tf_op jit(solution)/shard_map/psum | solution.py:61
Sparse Core Ops, SparseCore 0:
  38.1 57.7 all-gather.1
  150.1 150.3 reduce-scatter.1
  324.7 105.7 all-reduce.2
  433.0 247.9 all-reduce.4
